TPU v7x, 32 devices: a whole 2x2x4 slice. The times are simulated.
32 devices in a mesh: parts: 2 (over y), seq: 4 (over z), chan: 4 (over x, core).
Axes of the slice: x: 2, y: 2, z: 4, core: 2. Of those that a mesh axis runs over, the one named last changes fastest.
Arguments:
- x_tokens: bfloat16 [64, 8192], P(('parts', 'seq'), 'chan'), parts along dimension 0, may hold values from -6 to 6
- norm_gain: float32 [8192], P('chan'), may hold values from 0.5 to 1.5
- w_in: bfloat16 [3, 8192, 8192], P(None, 'seq', 'chan'), may hold values from -0.0625 to 0.0625
- short_filter: float32 [3, 3, 8192], P(None, None, 'seq'), may hold values from -3 to 3
- se_filter: float32 [7, 512], P(None, 'seq'), may hold values from -2 to 2
- w_out: bfloat16 [8192, 8192], P('seq'), may hold values from -0.0625 to 0.0625
Outputs:
- mixed_out: bfloat16 [64, 8192], P(('parts', 'chan'), 'seq'), parts along dimension 0
There are 2 independent parts, one for each index of `parts`. A program takes and returns all parts, laid end to end along the dimension named above; an argument that names none is the same for every part. Nothing has to cross between parts.
All inputs are finite; a program needn't handle non-finite values.
Results may differ from a plain program's by a relative error of at most 0.0086.
Values may be sent and summed in bfloat16 or wider, within the bound.
No kernel may reach another device: no remote copies, remote signals or barrier semaphores. Data moves between devices by JAX's collectives and lax.ppermute only.
A program may use at most 128 MiB of HBM per device.

v0:
```python
import jax
import jax.numpy as jnp
from jax import lax
from jax.sharding import PartitionSpec as P

D = 8192
GROUP = 16
epsilon = 1e-06


def from_behind(value, axis, steps):
    count = lax.axis_size(axis)
    leading, last = (max(0, -steps), min(count, count - steps))
    return lax.ppermute(value, axis, [(source, source + steps) for source in range(leading, last)])


def mixer(extended, short_taps, long_taps):
    wide = extended.astype(jnp.float32)
    row_count = wide.shape[0]
    featured = sum(
        (short_taps[offset] * wide[2 - offset : row_count - offset] for offset in range(3))
    )
    queries = featured[:, 0]
    product = featured[:, 1] * featured[:, 2]
    length = product.shape[0]
    filtered = sum(
        (long_taps[offset] * product[6 - offset : length - offset] for offset in range(7))
    )
    return (queries[6:] * filtered).astype(jnp.bfloat16)


def contract_last(left, right):
    return lax.dot_general(
        left, right, (((1,), (1,)), ((), ())), preferred_element_type=jnp.float32
    )


def shards(x_tokens, norm_gain, w_in, short_filter, se_filter, w_out):
    wide = x_tokens.astype(jnp.float32)
    local_squares = jnp.sum(wide * wide, axis=1, keepdims=True)
    total_squares = lax.psum(local_squares, "chan")
    factor = lax.rsqrt(total_squares / D + epsilon)
    normed = (wide * factor * norm_gain).astype(jnp.bfloat16)
    columns = w_in.shape[1]
    flat_in = w_in.reshape(3 * columns, w_in.shape[2])
    piece = lax.all_gather(normed, "seq", axis=0, tiled=True)
    partial_terms = contract_last(piece, flat_in).reshape(piece.shape[0], 3, columns)
    long_full = jnp.repeat(se_filter, GROUP, axis=1)
    mine = lax.psum_scatter(partial_terms, "chan", scatter_dimension=0, tiled=True).astype(
        jnp.bfloat16
    )
    previous = from_behind(mine[-8:], "chan", 1)
    extended = jnp.concatenate([previous, mine], axis=0)
    gated = mixer(extended, short_filter, long_full)
    result = contract_last(lax.all_gather(gated, "seq", axis=1, tiled=True), w_out)
    return result.astype(jnp.bfloat16)


def solution(mesh):
    placed = (
        P(("parts", "seq"), "chan"),
        P("chan"),
        P(None, "seq", "chan"),
        P(None, None, "seq"),
        P(None, "seq"),
        P("seq", None),
    )
    return jax.shard_map(
        shards, mesh=mesh, in_specs=placed, out_specs=P(("parts", "chan"), "seq"), check_vma=False
    )
```

profile of v0, /device:TPU:0, one launch (start us, length us, event | category | flops | bytes accessed | tf_op | source)
XLA Modules:
  0.0 107.5 jit_solution(7954886832939469192)
XLA Ops:
  6.5 0.0 reduce-scatter.2.cloned.1.call-start
  6.5 0.9 fusion.4
  7.4 8.4 %psum.7 = f32[8,1]{0,1:T(1,128)S(1)} all-reduce(f32[8,1]{0,1:T(1,128)S(1)} %bitcast.89), channel_id=1, replica_groups=mesh['parts'=2,'seq'=4,'chan'=4] {'chan'}, use_global_device_ids=true, to_apply=%region_1.0 | all-reduce | flops 8 | bytes 64 | tf_op jit(solution)/shard_map/psum | solution.py:41
  15.8 0.8 fusion.6
  16.6 13.6 %all_gather.6 = bf16[32,2048]{1,0:T(8,128)(2,1)S(1)} all-gather(bf16[8,2048]{1,0:T(8,128)(2,1)S(1)} %fusion.6), channel_id=1, replica_groups=mesh['parts'=2,'seq'=4,'chan'=4] {'seq'}, dimensions={0}, use_global_device_ids=true | all-gather | bytes 163840 | tf_op jit(solution)/shard_map/all_gather | solution.py:46
  30.2 13.0 %fusion.2 = f32[32,3,2048]{2,0,1:T(8,128)} fusion(bf16[3,2048,2048]{2,1,0:T(8,128)(2,1)} %param.8, bf16[32,2048]{1,0:T(8,128)(2,1)S(1)} %all_gather.6), kind=kOutput, calls=%fused_computation.8 | convolution fusion | flops 805306368 | bytes 26083328 | tf_op jit(solution)/shard_map/dot_general | solution.py:33
  43.3 0.0 reduce-scatter.2.cloned.1.call-update
  43.3 0.8 slice_bitcast_fusion.10
  44.1 22.8 %reduce-scatter.2.cloned.1.call-done = f32[8,3,2048]{2,0,1:T(8,128)} async-done(((f32[32,3,2048]{2,0,1:T(8,128)}), f32[8,3,2048]{2,0,1:T(8,128)}) %reduce-scatter.2.cloned.1.call-update) | async-done | bytes 196624 | tf_op jit(solution)/shard_map/reduce_scatter | solution.py:49
  66.9 0.9 convert_element_type.20
  67.9 1.6 %collective-permute-start = (bf16[8,3,2048]{2,0,1:T(8,128)(2,1)S(1)}, bf16[8,3,2048]{2,0,1:T(8,128)(2,1)S(1)}, u32[]{:S(2)}, u32[]{:S(2)}) collective-permute-start(bf16[8,3,2048]{2,0,1:T(8,128)(2,1)S(1)} %convert_element_type.20), channel_id=1, source_target_pairs={{0,1},{1,2},{2,3},{4,5},{5,6},{6,7},{8,9},{9,10},{10,11},{12,13},{... | collective-permute-start | bytes 294920 | tf_op jit(solution)/shard_map/ppermute | solution.py:14
  69.4 0.9 slice_bitcast_fusion.17
  70.4 0.1 broadcast_in_dim.34
  70.5 0.1 broadcast_in_dim.35
  70.6 0.1 broadcast_in_dim.36
  70.6 0.1 broadcast_in_dim.37
  70.7 0.1 broadcast_in_dim.38
  70.8 0.1 broadcast_in_dim.39
  70.9 0.1 broadcast_in_dim.40
  71.0 0.1 broadcast_in_dim.41
  71.1 0.1 broadcast_in_dim.42
  71.1 0.1 broadcast_in_dim.43
  71.2 0.1 broadcast_in_dim.44
  71.3 0.1 broadcast_in_dim.45
  71.4 0.1 broadcast_in_dim.46
  71.5 0.1 broadcast_in_dim.47
  71.6 0.0 collective-permute-done
  71.6 0.1 fusion
  71.8 0.1 fusion.10
  71.8 13.7 %all_gather.7 = bf16[8,8192]{1,0:T(8,128)(2,1)S(1)} all-gather(bf16[8,2048]{1,0:T(8,128)(2,1)S(1)} %fusion.10), channel_id=1, replica_groups=mesh['parts'=2,'seq'=4,'chan'=4] {'seq'}, dimensions={1}, use_global_device_ids=true | all-gather | bytes 163840 | tf_op jit(solution)/shard_map/all_gather | solution.py:55
  85.5 15.1 %convolution_convert_fusion = bf16[8,2048]{1,0:T(8,128)(2,1)} fusion(bf16[8,8192]{1,0:T(8,128)(2,1)S(1)} %all_gather.7, bf16[2048,8192]{1,0:T(8,128)(2,1)} %param.11), kind=kOutput, calls=%fused_computation | convolution fusion | flops 268451840 | bytes 33718272 | tf_op jit(solution)/shard_map/dot_general | solution.py:33
  (3 shorter events, 0.1 us)
Async XLA Ops:
  6.5 60.4 %reduce-scatter.2.cloned.1.call-start = ((), (), s32[]{:S(2)}) async-start(), calls=%async_computation.1 | async-start | bytes 983040 | tf_op jit(solution)/shard_map/reduce_scatter | solution.py:49
  67.9 3.7 %collective-permute-start = (bf16[8,3,2048]{2,0,1:T(8,128)(2,1)S(1)}, bf16[8,3,2048]{2,0,1:T(8,128)(2,1)S(1)}, u32[]{:S(2)}, u32[]{:S(2)}) collective-permute-start(bf16[8,3,2048]{2,0,1:T(8,128)(2,1)S(1)} %convert_element_type.20), channel_id=1, source_target_pairs={{0,1},{1,2},{2,3},{4,5},{5,6},{6,7},{8,9},{9,10},{10,11},{12,13},{... | collective-permute-start | bytes 294920 | tf_op jit(solution)/shard_map/ppermute | solution.py:14
Sparse Core Ops, SparseCore 0:
  43.4 23.4 reduce-scatter.1
where the time goes:
time: 108 us; the launch traced here: 107 us
  blocking collectives  35.7 us (33%)
  matrix products  28.1 us (26%)
  waiting for transfers between devices  22.8 us (21%)
  between operations  13.4 us (12%)
  local copies, waits for them, and re-layouts  2.93 us (3%)
  other arithmetic  2.92 us (3%)
  starting transfers between devices  1.56 us (1%)
    dot_general x2, matrix products, contract_last(): lax.dot_general(left, right, (((1,), (1,)), ((), ())), preferred_element_...  28.1 us
    reduce_scatter x1, waiting for transfers between devices, shards(): lax.psum_scatter(partial_terms, 'chan', scatter_dimension=0, tiled=True)  22.8 us
    all_gather x1, blocking collectives, shards(): lax.all_gather(gated, 'seq', axis=1, tiled=True)  13.7 us
    all_gather x1, blocking collectives, shards(): piece = lax.all_gather(normed, 'seq', axis=0, tiled=True)  13.6 us
    psum x1, blocking collectives, shards(): total_squares = lax.psum(local_squares, 'chan')  8.36 us
  transfers between devices with their start and end apart: 2, of which 1 were waited for; matrix products, arithmetic and copies ran while one was open for 3% of the time, Pallas kernels for 0%

commit v1 on v0

--- a/solution.py
+++ b/solution.py
@@ -52,7 +52,8 @@
     previous = from_behind(mine[-8:], "chan", 1)
     extended = jnp.concatenate([previous, mine], axis=0)
     gated = mixer(extended, short_filter, long_full)
-    result = contract_last(lax.all_gather(gated, "seq", axis=1, tiled=True), w_out)
+    _update_sites = lambda panel: jnp.concatenate(lax.all_gather(panel, "seq"), 1)
+    result = contract_last(_update_sites(gated), w_out)
     return result.astype(jnp.bfloat16)
 
 

time: 108 us -> 108 us (level)
  no operation moved by 1% of the time
where the time goes in v1:
time: 108 us; the launch traced here: 107 us
  blocking collectives  35.7 us (33%)
  matrix products  28.1 us (26%)
  waiting for transfers between devices  22.8 us (21%)
  between operations  13.4 us (12%)
  local copies, waits for them, and re-layouts  2.93 us (3%)
  other arithmetic  2.92 us (3%)
  starting transfers between devices  1.56 us (1%)
    dot_general x2, matrix products, contract_last(): lax.dot_general(left, right, (((1,), (1,)), ((), ())), preferred_element_...  28.1 us
    reduce_scatter x1, waiting for transfers between devices, shards(): lax.psum_scatter(partial_terms, 'chan', scatter_dimension=0, tiled=True)  22.8 us
    all_gather x1, blocking collectives, shards(): lax.all_gather(panel, 'seq')  13.7 us
    all_gather x1, blocking collectives, shards(): piece = lax.all_gather(normed, 'seq', axis=0, tiled=True)  13.6 us
    psum x1, blocking collectives, shards(): total_squares = lax.psum(local_squares, 'chan')  8.36 us
  transfers between devices with their start and end apart: 2, of which 1 were waited for; matrix products, arithmetic and copies ran while one was open for 3% of the time, Pallas kernels for 0%

profile of v1, /device:TPU:0, one launch (start us, length us, event | category | flops | bytes accessed | tf_op | source)
XLA Modules:
  0.0 107.5 jit_solution(4308337782355564800)
XLA Ops:
  6.5 0.0 reduce-scatter.2.cloned.1.call-start
  6.5 0.9 fusion.4
  7.4 8.4 %psum.7 = f32[8,1]{0,1:T(1,128)S(1)} all-reduce(f32[8,1]{0,1:T(1,128)S(1)} %bitcast.95), channel_id=1, replica_groups=mesh['parts'=2,'seq'=4,'chan'=4] {'chan'}, use_global_device_ids=true, to_apply=%region_1.0 | all-reduce | flops 8 | bytes 64 | tf_op jit(solution)/shard_map/psum | solution.py:41
  15.8 0.8 fusion.6
  16.6 13.6 %all_gather.9 = bf16[32,2048]{1,0:T(8,128)(2,1)S(1)} all-gather(bf16[8,2048]{1,0:T(8,128)(2,1)S(1)} %fusion.6), channel_id=1, replica_groups=mesh['parts'=2,'seq'=4,'chan'=4] {'seq'}, dimensions={0}, use_global_device_ids=true | all-gather | bytes 163840 | tf_op jit(solution)/shard_map/all_gather | solution.py:46
  30.2 13.0 %fusion.2 = f32[32,3,2048]{2,0,1:T(8,128)} fusion(bf16[3,2048,2048]{2,1,0:T(8,128)(2,1)} %param.8, bf16[32,2048]{1,0:T(8,128)(2,1)S(1)} %all_gather.9), kind=kOutput, calls=%fused_computation.8 | convolution fusion | flops 805306368 | bytes 26083328 | tf_op jit(solution)/shard_map/dot_general | solution.py:33
  43.3 0.0 reduce-scatter.2.cloned.1.call-update
  43.3 0.8 slice_bitcast_fusion.10
  44.1 22.8 %reduce-scatter.2.cloned.1.call-done = f32[8,3,2048]{2,0,1:T(8,128)} async-done(((f32[32,3,2048]{2,0,1:T(8,128)}), f32[8,3,2048]{2,0,1:T(8,128)}) %reduce-scatter.2.cloned.1.call-update) | async-done | bytes 196624 | tf_op jit(solution)/shard_map/reduce_scatter | solution.py:49
  66.9 0.9 convert_element_type.20
  67.9 1.6 %collective-permute-start = (bf16[8,3,2048]{2,0,1:T(8,128)(2,1)S(1)}, bf16[8,3,2048]{2,0,1:T(8,128)(2,1)S(1)}, u32[]{:S(2)}, u32[]{:S(2)}) collective-permute-start(bf16[8,3,2048]{2,0,1:T(8,128)(2,1)S(1)} %convert_element_type.20), channel_id=1, source_target_pairs={{0,1},{1,2},{2,3},{4,5},{5,6},{6,7},{8,9},{9,10},{10,11},{12,13},{... | collective-permute-start | bytes 294920 | tf_op jit(solution)/shard_map/ppermute | solution.py:14
  69.4 0.9 slice_bitcast_fusion.17
  70.4 0.1 broadcast_in_dim.34
  70.5 0.1 broadcast_in_dim.35
  70.6 0.1 broadcast_in_dim.36
  70.6 0.1 broadcast_in_dim.37
  70.7 0.1 broadcast_in_dim.38
  70.8 0.1 broadcast_in_dim.39
  70.9 0.1 broadcast_in_dim.40
  71.0 0.1 broadcast_in_dim.41
  71.1 0.1 broadcast_in_dim.42
  71.1 0.1 broadcast_in_dim.43
  71.2 0.1 broadcast_in_dim.44
  71.3 0.1 broadcast_in_dim.45
  71.4 0.1 broadcast_in_dim.46
  71.5 0.1 broadcast_in_dim.47
  71.6 0.0 collective-permute-done
  71.6 0.1 fusion
  71.8 0.1 fusion.10
  71.8 13.7 %all-gather = bf16[32,2048]{1,0:T(8,128)(2,1)S(1)} all-gather(bf16[8,2048]{1,0:T(8,128)(2,1)S(1)} %fusion.10), channel_id=2, replica_groups=mesh['parts'=2,'seq'=4,'chan'=4] {'seq'}, dimensions={0}, use_global_device_ids=true | all-gather | bytes 163840 | tf_op jit(solution)/shard_map/all_gather | solution.py:55
  85.5 15.1 %convolution_convert_fusion = bf16[8,2048]{1,0:T(8,128)(2,1)} fusion(bf16[8,8192]{1,0:T(8,128)(2,1)S(1)} %bitcast.94, bf16[2048,8192]{1,0:T(8,128)(2,1)} %param.11), kind=kOutput, calls=%fused_computation | convolution fusion | flops 268451840 | bytes 33718272 | tf_op jit(solution)/shard_map/dot_general | solution.py:33
  (3 shorter events, 0.1 us)
Async XLA Ops:
  6.5 60.4 %reduce-scatter.2.cloned.1.call-start = ((), (), s32[]{:S(2)}) async-start(), calls=%async_computation.1 | async-start | bytes 983040 | tf_op jit(solution)/shard_map/reduce_scatter | solution.py:49
  67.9 3.7 %collective-permute-start = (bf16[8,3,2048]{2,0,1:T(8,128)(2,1)S(1)}, bf16[8,3,2048]{2,0,1:T(8,128)(2,1)S(1)}, u32[]{:S(2)}, u32[]{:S(2)}) collective-permute-start(bf16[8,3,2048]{2,0,1:T(8,128)(2,1)S(1)} %convert_element_type.20), channel_id=1, source_target_pairs={{0,1},{1,2},{2,3},{4,5},{5,6},{6,7},{8,9},{9,10},{10,11},{12,13},{... | collective-permute-start | bytes 294920 | tf_op jit(solution)/shard_map/ppermute | solution.py:14
Sparse Core Ops, SparseCore 0:
  43.4 23.4 reduce-scatter.1
